TPU v7x, 256 devices: a whole 4x4x8 slice. The times are simulated.
256 devices in a mesh: period: 128 (over z, x, y), half: 2 (over core).
Axes of the slice: x: 4, y: 4, z: 8, core: 2. Of those that a mesh axis runs over, the one named last changes fastest.
Arguments:
- probes: float32 [1024, 4, 512], P('period', None, 'half'), may hold values from -6 to 6
- footprints: bfloat16 [1024, 512, 512], P('period', None, 'half'), may hold values from -0.25 to 0.25
- lag_weights: float32 [1024, 4], P('period'), may hold values from 0.2 to 2
- owners: int32 [1024, 4], P('period'), may hold values from 0 to 127, all different within a row; in each aligned block of 8 rows (0 to 7, 8 to 15, ...) at most 2 rows name the same one
- window_tiles: int32 [1024, 2], P('period', 'half'), may hold values from 0 to 10
- coords: int32 [2, 3072], replicated, may hold values from 0 to 63
- temporal: float32 [128, 128], replicated, as said below
Outputs:
- coefficients: float32 [4, 4], replicated
- residual: float32 [1024, 4, 512], P('period', None, 'half')
Inputs may be any that keep to these rules, and one draw needn't show every extreme that they name: `owners`: each row names 4 different periods. Among the 8 rows of one index of period, no period is named more than 2 times, and one is named exactly 2 times. `temporal`: symmetric.
All inputs are finite; a program needn't handle non-finite values.
Results may differ from a plain program's by a relative error of at most 0.025.
Values may be sent and summed in bfloat16 or wider, within the bound.
No kernel may reach another device: no remote copies, remote signals or barrier semaphores. Data moves between devices by JAX's collectives and lax.ppermute only.
A program may use at most 64 MiB of HBM per device.

v0:
```python
import jax
import jax.numpy as jnp
from jax import lax
from jax.sharding import PartitionSpec as P

epsilon = 1e-06
kernel_scale = 0.05
kernel_length = 6.0
highest = lax.Precision.HIGHEST


def from_partner(block, axis, bit):
    count = lax.axis_size(axis)
    route = []
    for low in range(count):
        high = low | 1 << bit
        if high != low and high < count:
            route += [(low, high), (high, low)]
    return lax.ppermute(block, axis, route)


def body(probes, footprints, lag_weights, owners, window_tiles, coords, temporal):
    periods = lax.axis_size("period")
    half_index = lax.axis_index("half")
    block_count, top_count = owners.shape
    probe_count = probes.shape[1]
    sound_count = footprints.shape[1]
    window = footprints.shape[2]
    win_tiles = window // 128
    cell_count = coords.shape[1]
    half_cells = cell_count // 2
    tile_count = half_cells // 128
    group_cells = half_cells // periods
    total_rows = float(block_count * periods * sound_count)
    tiles = window_tiles[:, 0]
    tile_hot = (
        tiles[:, None, None] + jnp.arange(win_tiles, dtype=jnp.int32)[None, :, None]
        == jnp.arange(tile_count, dtype=jnp.int32)[None, None, :]
    ).astype(jnp.float32)
    own_coords = lax.dynamic_slice_in_dim(coords, half_index * half_cells, half_cells, 1)
    delta_x = own_coords[0][:, None] - coords[0][None, :]
    delta_y = own_coords[1][:, None] - coords[1][None, :]
    squared = (delta_x * delta_x + delta_y * delta_y).astype(jnp.float32)
    kernel_rows = (kernel_scale * jnp.exp(-jnp.sqrt(squared) / kernel_length)).reshape(
        periods, group_cells, cell_count
    )
    owner_hot = (owners[:, :, None] == jnp.arange(periods, dtype=jnp.int32)[None, None, :]).astype(
        jnp.float32
    )

    def add_half(piece_rows):
        return jnp.einsum(
            "bps,bsw->bpw", piece_rows, footprints, preferred_element_type=jnp.float32
        )

    def mix_periods(grouped_part):
        mixed_part = jnp.einsum("ts,sik->tik", temporal, grouped_part, precision=highest)
        return lax.all_to_all(mixed_part, "period", split_axis=0, concat_axis=0, tiled=True)

    def apply_operator(vector):
        vector_low = vector.astype(jnp.bfloat16)
        partial_value = add_half(lax.all_gather(vector_low, "half", axis=2, tiled=True))
        terms = lag_weights[:, :, None, None] * partial_value[:, None, :, :]
        term_tiles = terms.reshape(block_count, top_count, probe_count, win_tiles, 128)
        placed = jnp.einsum("bjt,bkpjl->bkptl", tile_hot, term_tiles, precision=highest)
        dense_terms = jnp.einsum("bkn,bkptl->nptl", owner_hot, placed, precision=highest)
        summed = lax.psum_scatter(
            dense_terms.reshape(periods, probe_count, half_cells),
            "period",
            scatter_dimension=0,
            tiled=True,
        )
        flux_half = summed[0]
        other_half = from_partner(flux_half, "half", 0)
        whole_flux = jnp.where(
            half_index == 0,
            jnp.concatenate([flux_half, other_half], axis=1),
            jnp.concatenate([other_half, flux_half], axis=1),
        )
        grouped = jnp.einsum("pc,gkc->gpk", whole_flux, kernel_rows, precision=highest)
        mixed_flux = mix_periods(
            lax.all_to_all(grouped, "period", split_axis=0, concat_axis=0, tiled=True)
        )
        field_low = (
            jnp.transpose(mixed_flux, (1, 0, 2))
            .reshape(probe_count, half_cells)
            .astype(jnp.bfloat16)
        )
        field_all = lax.all_gather(field_low[None], "period", axis=0, tiled=True)
        selected = jnp.einsum(
            "bkn,npc->bkpc",
            owner_hot.astype(jnp.bfloat16),
            field_all,
            preferred_element_type=jnp.float32,
        )
        selected = selected.reshape(block_count, top_count, probe_count, tile_count, 128)
        windows = jnp.einsum("bkptl,bjt->bkpjl", selected, tile_hot, precision=highest)
        windows = windows.astype(jnp.bfloat16).reshape(block_count, top_count, probe_count, window)
        products = jnp.einsum(
            "bkpw,bsw->bkps", windows, footprints, preferred_element_type=jnp.float32
        )
        sounded = jnp.einsum("bk,bkps->bps", lag_weights, products, precision=highest)
        return lax.psum_scatter(
            sounded.astype(jnp.bfloat16), "half", scatter_dimension=2, tiled=True
        ).astype(jnp.float32)

    def local_mean(values):
        return jnp.sum(values, axis=(0, 2))

    def lanczos_step(current, image):
        inner_sum = lax.psum(local_mean(current * image), ("period", "half"))
        alpha = inner_sum / total_rows
        remainder = image - alpha[None, :, None] * current
        square_sum = lax.psum(local_mean(remainder * remainder), ("period", "half"))
        beta = jnp.sqrt(square_sum / total_rows + epsilon)
        return (alpha, remainder, beta)

    start_sum = lax.psum(local_mean(probes * probes), ("period", "half"))
    first_q = probes / jnp.sqrt(start_sum / total_rows + epsilon)[None, :, None]
    image_one = apply_operator(first_q)
    alpha_one, rest_one, beta_one = lanczos_step(first_q, image_one)
    second_q = rest_one / beta_one[None, :, None]
    image_two = apply_operator(second_q) - beta_one[None, :, None] * first_q
    alpha_two, residual, beta_two = lanczos_step(second_q, image_two)
    coefficients = jnp.stack([alpha_one, beta_one, alpha_two, beta_two], axis=0)
    return (coefficients, residual)


def solution(mesh):
    in_specs = (
        P("period", None, "half"),
        P("period", None, "half"),
        P("period", None),
        P("period", None),
        P("period", "half"),
        P(),
        P(),
    )
    out_specs = (P(), P("period", None, "half"))
    return jax.shard_map(body, mesh=mesh, in_specs=in_specs, out_specs=out_specs, check_vma=False)
```

profile of v0, /device:TPU:1, one launch (start us, length us, event | category | flops | bytes accessed | tf_op | source)
XLA Modules:
  0.0 1305.8 jit_solution(13119377155676004425)
XLA Ops:
  7.2 1.0 multiply_reduce_fusion.3
  8.3 81.4 %psum.35 = f32[4]{0:T(128)S(1)} all-reduce(f32[4]{0:T(128)S(1)} %multiply_reduce_fusion.3), channel_id=1, replica_groups=mesh['period'=128,'half'=2] {'period','half'}, use_global_device_ids=true, to_apply=%region_1.0 | all-reduce | flops 4 | bytes 32 | tf_op jit(solution)/shard_map/psum | solution.py:118
  89.7 0.7 iota_add_fusion
  90.4 0.8 copy.24
  91.2 0.8 fusion.101
  92.0 2.5 all_gather.12
  94.9 0.8 convolution_bitcast_fusion.1
  95.7 4.4 fusion.38
  100.1 5.1 copy.26
  106.4 221.5 %all-reduce.5.cloned.1.call-done = f32[128,4,1536]{2,1,0:T(4,128)} async-done(((f32[128,4,1536]{2,1,0:T(4,128)}), f32[128,4,1536]{2,1,0:T(4,128)}) %all-reduce.5.cloned.1.call-update) | async-done | bytes 3145744
  328.0 1.4 dynamic-slice_bitcast_fusion.1
  329.4 4.9 collective-permute-start
  335.2 46.6 %fusion.32 = f32[128,4,12]{0,1,2:T(4,128)S(1)} fusion(s32[3072]{0:T(1024)S(1)} %bitcast.132, s32[128,12]{0,1:T(8,128)S(1)} %copy.23, s32[3072]{0:T(1024)S(1)} %bitcast.130, s32[128,12]{0,1:T(8,128)S(1)} %copy.22, f32[4,1536]{1,0:T(4,128)S(1)} %collective-permute-done, f32[4,1536]{1,0:T(4,128)S(1)} %dynamic-slice_bitcast_fusion.1, pred[]{:T(512)S(6)} %eq.36), kind=kOutput, calls=%fused_computation.35 | convolution fusion | flops 268996608 | bytes 110593 | tf_op jit(solution)/shard_map/pc,gkc->gpk/dot_general | solution.py:80
  382.0 23.7 %all_to_all.20 = f32[128,4,12]{2,1,0:T(4,128)S(1)} all-to-all(f32[128,4,12]{2,1,0:T(4,128)S(1)} %copy.27), channel_id=1, replica_groups=mesh['period'=128,'half'=2] {'period'}, dimensions={0} | all-to-all | bytes 49152 | tf_op jit(solution)/shard_map/all_to_all | solution.py:82
  406.4 17.2 %all_to_all.21 = bf16[128,4,12]{2,1,0:T(4,128)(2,1)S(1)} all-to-all(bf16[128,4,12]{2,1,0:T(4,128)(2,1)S(1)} %copy.29), channel_id=1, replica_groups=mesh['period'=128,'half'=2] {'period'}, dimensions={0} | all-to-all | bytes 24576 | tf_op jit(solution)/shard_map/all_to_all | solution.py:58
  423.7 0.8 convert_element_type.80
  424.8 94.2 %all-gather.3.cloned.1.call-done = bf16[128,4,1536]{2,1,0:T(4,128)(2,1)} async-done(((bf16[1,4,1536]{2,1,0:T(4,128)(2,1)}), bf16[128,4,1536]{2,1,0:T(4,128)(2,1)}) %all-gather.3.cloned.1.call-update) | async-done | bytes 1572880 | tf_op jit(solution)/shard_map/all_gather | solution.py:89
  519.0 2.0 fusion.24
  521.7 0.6 fusion.16
  522.3 0.6 fusion.42
  523.0 0.7 copy.52
  523.7 1.3 reshape.130
  525.1 16.9 %reduce-scatter.7.cloned.1.call-done = bf16[256,32]{1,0:T(8,128)(2,1)} async-done(((bf16[512,32]{1,0:T(8,128)(2,1)}), bf16[256,32]{1,0:T(8,128)(2,1)}) %reduce-scatter.7.cloned.1.call-update) | async-done | bytes 16400
  542.0 1.2 reshape.131
  543.7 77.4 %psum.36 = f32[4]{0:T(128)S(1)} all-reduce(f32[4]{0:T(128)S(1)} %fusion.68), channel_id=1, replica_groups=mesh['period'=128,'half'=2] {'period','half'}, use_global_device_ids=true, to_apply=%region_5.6 | all-reduce | flops 4 | bytes 32 | tf_op jit(solution)/shard_map/psum | solution.py:111
  621.3 73.1 %psum.37 = f32[4]{0:T(128)S(1)} all-reduce(f32[4]{0:T(128)S(1)} %multiply_reduce_fusion.2), channel_id=1, replica_groups=mesh['period'=128,'half'=2] {'period','half'}, use_global_device_ids=true, to_apply=%region_7.8 | all-reduce | flops 4 | bytes 32 | tf_op jit(solution)/shard_map/psum | solution.py:114
  694.5 2.2 all_gather.14
  697.1 0.8 convolution_bitcast_fusion
  697.9 4.4 fusion.36
  702.3 5.1 copy.34
  707.5 223.8 %all-reduce.7.cloned.1.call-done = f32[128,4,1536]{2,1,0:T(4,128)} async-done(((f32[128,4,1536]{2,1,0:T(4,128)}), f32[128,4,1536]{2,1,0:T(4,128)}) %all-reduce.7.cloned.1.call-update) | async-done | bytes 3145744
  931.3 1.4 dynamic-slice_bitcast_fusion
  932.7 4.9 collective-permute-start.1
  937.6 0.8 collective-permute-done.1
  938.5 46.6 %fusion.33 = f32[128,4,12]{0,1,2:T(4,128)S(1)} fusion(s32[3072]{0:T(1024)S(1)} %bitcast.133, s32[128,12]{0,1:T(8,128)S(1)} %copy.23, s32[3072]{0:T(1024)S(1)} %bitcast.131, s32[128,12]{0,1:T(8,128)S(1)} %copy.22, f32[4,1536]{1,0:T(4,128)S(1)} %collective-permute-done.1, f32[4,1536]{1,0:T(4,128)S(1)} %dynamic-slice_bitcast_fusion, pred[]{:T(512)S(6)} %eq.36), kind=kOutput, calls=%fused_computation.36 | convolution fusion | flops 268996608 | bytes 110593 | tf_op jit(solution)/shard_map/pc,gkc->gpk/dot_general | solution.py:80
  985.3 23.7 %all_to_all.22 = f32[128,4,12]{2,1,0:T(4,128)S(1)} all-to-all(f32[128,4,12]{2,1,0:T(4,128)S(1)} %copy.35), channel_id=1, replica_groups=mesh['period'=128,'half'=2] {'period'}, dimensions={0} | all-to-all | bytes 49152 | tf_op jit(solution)/shard_map/all_to_all | solution.py:82
  1009.7 17.2 %all_to_all.23 = bf16[128,4,12]{2,1,0:T(4,128)(2,1)S(1)} all-to-all(bf16[128,4,12]{2,1,0:T(4,128)(2,1)S(1)} %copy.37), channel_id=1, replica_groups=mesh['period'=128,'half'=2] {'period'}, dimensions={0} | all-to-all | bytes 24576 | tf_op jit(solution)/shard_map/all_to_all | solution.py:58
  1027.0 0.8 convert_element_type.88
  1027.9 94.5 %all-gather.5.cloned.1.call-done = bf16[128,4,1536]{2,1,0:T(4,128)(2,1)} async-done(((bf16[1,4,1536]{2,1,0:T(4,128)(2,1)}), bf16[128,4,1536]{2,1,0:T(4,128)(2,1)}) %all-gather.5.cloned.1.call-update) | async-done | bytes 1572880 | tf_op jit(solution)/shard_map/all_gather | solution.py:89
  1122.3 2.0 fusion.27
  1125.0 0.6 fusion.14
  1126.3 0.7 copy.54
  1127.0 1.3 reshape.132
  1128.4 16.9 %reduce-scatter.9.cloned.1.call-done = bf16[256,32]{1,0:T(8,128)(2,1)} async-done(((bf16[512,32]{1,0:T(8,128)(2,1)}), bf16[256,32]{1,0:T(8,128)(2,1)}) %reduce-scatter.9.cloned.1.call-update) | async-done | bytes 16400
  1145.3 1.2 reshape.133
  1147.0 77.4 %psum.38 = f32[4]{0:T(128)S(1)} all-reduce(f32[4]{0:T(128)S(1)} %multiply_reduce_fusion.1), channel_id=1, replica_groups=mesh['period'=128,'half'=2] {'period','half'}, use_global_device_ids=true, to_apply=%region_11.12 | all-reduce | flops 4 | bytes 32 | tf_op jit(solution)/shard_map/psum | solution.py:111
  1224.5 0.8 multiply_reduce_fusion
  1225.3 73.1 %psum.39 = f32[4]{0:T(128)S(1)} all-reduce(f32[4]{0:T(128)S(1)} %get-tuple-element.4), channel_id=1, replica_groups=mesh['period'=128,'half'=2] {'period','half'}, use_global_device_ids=true, to_apply=%region_13.14 | all-reduce | flops 4 | bytes 32 | tf_op jit(solution)/shard_map/psum | solution.py:114
  (64 shorter events, 9.1 us)
Async XLA Ops:
  7.2 87.3 %copy-start = (bf16[8,512,256]{2,1,0:T(8,128)(2,1)S(1)}, bf16[8,512,256]{2,1,0:T(8,128)(2,1)}, u32[]{:S(2)}) copy-start(bf16[8,512,256]{2,1,0:T(8,128)(2,1)} %param.8) | copy-start | bytes 6291460
  7.2 88.5 %copy-start.3 = (s32[8,4]{0,1:T(4,128)S(1)}, s32[8,4]{0,1:T(4,128)}, u32[]{:S(2)}) copy-start(s32[8,4]{0,1:T(4,128)} %param.10) | copy-start | bytes 388
  7.2 320.8 %all-reduce.5.cloned.1.call-start = ((), (), s32[]{:S(2)}) async-start(), calls=%async_computation.10 | async-start | bytes 6291456
  105.2 0.7 copy-start.5
  105.2 229.1 %copy-start.2 = (s32[2,3072]{1,0:T(2,128)S(1)}, s32[2,3072]{1,0:T(2,128)}, u32[]{:S(2)}) copy-start(s32[2,3072]{1,0:T(2,128)} %param.12) | copy-start | bytes 73732
  105.2 413.8 %all-gather.3.cloned.1.call-start = ((), (), s32[]{:S(2)}) async-start(), calls=%async_computation.6 | async-start | bytes 1585152 | tf_op jit(solution)/shard_map/all_gather | solution.py:89
  329.4 5.8 collective-permute-start
  335.2 70.5 %copy-start.1 = (f32[128,128]{1,0:T(8,128)S(1)}, f32[128,128]{1,0:T(8,128)}, u32[]{:S(2)}) copy-start(f32[128,128]{1,0:T(8,128)} %param.13) | copy-start | bytes 196612
  335.2 89.6 %copy-start.4 = (f32[8,4]{0,1:T(4,128)S(1)}, f32[8,4]{0,1:T(4,128)}, u32[]{:S(2)}) copy-start(f32[8,4]{0,1:T(4,128)} %param.9) | copy-start | bytes 388
  424.5 117.5 %reduce-scatter.7.cloned.1.call-start = ((), (), s32[]{:S(2)}) async-start(), calls=%async_computation.8 | async-start | bytes 196608
  525.0 406.2 %all-reduce.7.cloned.1.call-start = ((), (), s32[]{:S(2)}) async-start(), calls=%async_computation.11 | async-start | bytes 6291456
  707.4 414.9 %all-gather.5.cloned.1.call-start = ((), (), s32[]{:S(2)}) async-start(), calls=%async_computation.7 | async-start | bytes 1585152 | tf_op jit(solution)/shard_map/all_gather | solution.py:89
  932.7 5.8 collective-permute-start.1
  1027.8 117.5 %reduce-scatter.9.cloned.1.call-start = ((), (), s32[]{:S(2)}) async-start(), calls=%async_computation.9 | async-start | bytes 196608
Sparse Core Ops, SparseCore 0:
  105.3 222.5 all-reduce.4
  424.6 94.3 all-gather.2
  525.2 16.7 reduce-scatter.6
  707.5 223.6 all-reduce.6
  1027.9 94.3 all-gather.4
  1128.5 16.7 reduce-scatter.8
where the time goes:
time: 1310 us
  waiting for transfers between devices  669 us (51%)
  blocking collectives  469 us (36%)
  matrix products  113 us (9%)
  local copies, waits for them, and re-layouts  25.2 us (2%)
  between operations  14.4 us (1%)
    unnamed x10, waiting for transfers between devices  479 us
    all_gather x2, waiting for transfers between devices, apply_operator(): field_all = lax.all_gather(field_low[None], 'period', axis=0, tiled=True)  189 us
    psum x2, blocking collectives, lanczos_step(): inner_sum = lax.psum(local_mean(current * image), ('period', 'half'))  155 us
    psum x2, blocking collectives, lanczos_step(): square_sum = lax.psum(local_mean(remainder * remainder), ('period', 'half'))  146 us
    dot_general x2, matrix products, apply_operator(): jnp.einsum('pc,gkc->gpk', whole_flux, kernel_rows, precision=highest)  93.3 us
    psum x1, blocking collectives, body(): start_sum = lax.psum(local_mean(probes * probes), ('period', 'half'))  81.4 us
    all_to_all x2, blocking collectives, apply_operator(): lax.all_to_all(grouped, 'period', split_axis=0, concat_axis=0, tiled=True)  47.4 us
    all_to_all x2, blocking collectives, mix_periods(): lax.all_to_all(mixed_part, 'period', split_axis=0, concat_axis=0, tiled=T...  34.5 us
  transfers between devices with their start and end apart: 8, of which 8 were waited for; matrix products, arithmetic and copies ran while one was open for 0% of the time, Pallas kernels for 0%

commit v1 on v0

--- a/solution.py
+++ b/solution.py
@@ -86,7 +86,10 @@
             .reshape(probe_count, half_cells)
             .astype(jnp.bfloat16)
         )
-        field_all = lax.all_gather(field_low[None], "period", axis=0, tiled=True)
+        field_all = jnp.concatenate(
+            lax.all_to_all(jnp.stack([field_low[None]] * lax.axis_size("period")), "period", 0, 0),
+            axis=0,
+        )
         selected = jnp.einsum(
             "bkn,npc->bkpc",
             owner_hot.astype(jnp.bfloat16),

time: 1310 us -> 1210 us (0.924)
  waiting for transfers between devices: 669 us -> 509 us
  blocking collectives: 469 us -> 512 us
    all_gather x2 -> x0, waiting for transfers between devices: 189 us -> none  [apply_operator(): field_all = lax.all_gather(field_low[None], 'period', axis=0, tiled=True)]
    all_to_all x0 -> x1, blocking collectives: none -> 43.1 us  [apply_operator(): lax.all_to_all(jnp.stack([field_low[None]] * lax.axis_size('period')), 'p...]
    all_to_all x0 -> x1, waiting for transfers between devices: none -> 36.4 us  [apply_operator(): lax.all_to_all(jnp.stack([field_low[None]] * lax.axis_size('period')), 'p...]
    unnamed x10 -> x8, waiting for transfers between devices: 479 us -> 471 us
  transfers between devices with their start and end apart: 8 -> 7, of which waited for: 8 -> 7; matrix products, arithmetic and copies ran while one was open for 0% -> 0% of each run, Pallas kernels for 0% -> 0%
where the time goes in v1:
time: 1210 us; the launch traced here: 1200 us
  blocking collectives  512 us (42%)
  waiting for transfers between devices  509 us (42%)
  matrix products  113 us (9%)
  local copies, waits for them, and re-layouts  33.8 us (3%)
  starting transfers between devices  17.7 us (1%)
  between operations  14.4 us (1%)
    unnamed x8, waiting for transfers between devices  471 us
    psum x2, blocking collectives, lanczos_step(): inner_sum = lax.psum(local_mean(current * image), ('period', 'half'))  155 us
    psum x2, blocking collectives, lanczos_step(): square_sum = lax.psum(local_mean(remainder * remainder), ('period', 'half'))  146 us
    dot_general x2, matrix products, apply_operator(): jnp.einsum('pc,gkc->gpk', whole_flux, kernel_rows, precision=highest)  93.3 us
    psum x1, blocking collectives, body(): start_sum = lax.psum(local_mean(probes * probes), ('period', 'half'))  81.4 us
    all_to_all x2, blocking collectives, apply_operator(): lax.all_to_all(grouped, 'period', split_axis=0, concat_axis=0, tiled=True)  47.4 us
    all_to_all x1, blocking collectives, apply_operator(): lax.all_to_all(jnp.stack([field_low[None]] * lax.axis_size('period')), 'p...  43.1 us
    all_to_all x1, waiting for transfers between devices, apply_operator(): lax.all_to_all(jnp.stack([field_low[None]] * lax.axis_size('period')), 'p...  36.4 us
  transfers between devices with their start and end apart: 7, of which 7 were waited for; matrix products, arithmetic and copies ran while one was open for 0% of the time, Pallas kernels for 0%

profile of v1, /device:TPU:1, one launch (start us, length us, event | category | flops | bytes accessed | tf_op | source)
XLA Modules:
  0.0 1204.6 jit_solution(6609845341051771960)
XLA Ops:
  7.2 1.0 multiply_reduce_fusion.3
  8.3 81.4 %psum.35 = f32[4]{0:T(128)S(1)} all-reduce(f32[4]{0:T(128)S(1)} %multiply_reduce_fusion.3), channel_id=1, replica_groups=mesh['period'=128,'half'=2] {'period','half'}, use_global_device_ids=true, to_apply=%region_1.0 | all-reduce | flops 4 | bytes 32 | tf_op jit(solution)/shard_map/psum | solution.py:121
  89.7 0.7 iota_add_fusion
  90.4 0.8 copy.18
  91.1 0.8 fusion.91
  92.0 2.5 all_gather.6
  94.9 0.8 convolution_bitcast_fusion.1
  95.7 4.4 fusion.26
  100.1 5.1 copy.20
  105.2 0.6 copy-done.5
  106.4 221.5 %all-reduce.5.cloned.1.call-done = f32[128,4,1536]{2,1,0:T(4,128)} async-done(((f32[128,4,1536]{2,1,0:T(4,128)}), f32[128,4,1536]{2,1,0:T(4,128)}) %all-reduce.5.cloned.1.call-update) | async-done | bytes 3145744
  327.9 1.4 dynamic-slice_bitcast_fusion.1
  329.3 4.9 collective-permute-start
  335.1 46.6 %fusion.20 = f32[128,4,12]{0,1,2:T(4,128)S(1)} fusion(s32[3072]{0:T(1024)S(1)} %bitcast.136, s32[128,12]{0,1:T(8,128)S(1)} %copy.17, s32[3072]{0:T(1024)S(1)} %bitcast.134, s32[128,12]{0,1:T(8,128)S(1)} %copy.16, f32[4,1536]{1,0:T(4,128)S(1)} %collective-permute-done, f32[4,1536]{1,0:T(4,128)S(1)} %dynamic-slice_bitcast_fusion.1, pred[]{:T(512)S(6)} %eq.36), kind=kOutput, calls=%fused_computation.27 | convolution fusion | flops 268996608 | bytes 110593 | tf_op jit(solution)/shard_map/pc,gkc->gpk/dot_general | solution.py:80
  381.9 23.7 %all_to_all.30 = f32[128,4,12]{2,1,0:T(4,128)S(1)} all-to-all(f32[128,4,12]{2,1,0:T(4,128)S(1)} %copy.21), channel_id=1, replica_groups=mesh['period'=128,'half'=2] {'period'}, dimensions={0} | all-to-all | bytes 49152 | tf_op jit(solution)/shard_map/all_to_all | solution.py:82
  406.4 17.2 %all_to_all.31 = bf16[128,4,12]{2,1,0:T(4,128)(2,1)S(1)} all-to-all(bf16[128,4,12]{2,1,0:T(4,128)(2,1)S(1)} %copy.23), channel_id=1, replica_groups=mesh['period'=128,'half'=2] {'period'}, dimensions={0} | all-to-all | bytes 24576 | tf_op jit(solution)/shard_map/all_to_all | solution.py:58
  423.8 1.6 stack.21
  425.4 7.4 all-to-all-start.2
  433.0 36.4 %all-to-all-done.2 = bf16[128,1,4,1536]{3,2,1,0:T(4,128)(2,1)} async-done(((bf16[128,1,4,1536]{3,2,1,0:T(4,128)(2,1)}), bf16[128,1,4,1536]{3,2,1,0:T(4,128)(2,1)}, u32[]{:S(2)}, u32[]{:S(2)}) %all-to-all-start.2) | async-done | bytes 1572896 | tf_op jit(solution)/shard_map/all_to_all | solution.py:90
  469.4 3.9 copy.25
  473.2 2.0 fusion.70
  477.2 0.7 copy.46
  477.9 1.3 reshape.130
  479.3 12.9 %reduce-scatter.7.cloned.1.call-done = bf16[256,32]{1,0:T(8,128)(2,1)} async-done(((bf16[512,32]{1,0:T(8,128)(2,1)}), bf16[256,32]{1,0:T(8,128)(2,1)}) %reduce-scatter.7.cloned.1.call-update) | async-done | bytes 16400
  492.2 1.2 reshape.131
  493.9 77.4 %psum.36 = f32[4]{0:T(128)S(1)} all-reduce(f32[4]{0:T(128)S(1)} %fusion.56), channel_id=1, replica_groups=mesh['period'=128,'half'=2] {'period','half'}, use_global_device_ids=true, to_apply=%region_5.6 | all-reduce | flops 4 | bytes 32 | tf_op jit(solution)/shard_map/psum | solution.py:114
  571.5 73.1 %psum.37 = f32[4]{0:T(128)S(1)} all-reduce(f32[4]{0:T(128)S(1)} %multiply_reduce_fusion.2), channel_id=1, replica_groups=mesh['period'=128,'half'=2] {'period','half'}, use_global_device_ids=true, to_apply=%region_7.8 | all-reduce | flops 4 | bytes 32 | tf_op jit(solution)/shard_map/psum | solution.py:117
  644.8 2.2 all_gather.7
  647.4 0.8 convolution_bitcast_fusion
  648.2 4.4 fusion.24
  652.6 5.1 copy.28
  657.7 223.8 %all-reduce.7.cloned.1.call-done = f32[128,4,1536]{2,1,0:T(4,128)} async-done(((f32[128,4,1536]{2,1,0:T(4,128)}), f32[128,4,1536]{2,1,0:T(4,128)}) %all-reduce.7.cloned.1.call-update) | async-done | bytes 3145744
  881.5 1.4 dynamic-slice_bitcast_fusion
  882.9 5.1 collective-permute-start.1
  888.1 0.8 collective-permute-done.1
  888.9 46.6 %fusion.21 = f32[128,4,12]{0,1,2:T(4,128)S(1)} fusion(s32[3072]{0:T(1024)S(1)} %bitcast.137, s32[128,12]{0,1:T(8,128)S(1)} %copy.17, s32[3072]{0:T(1024)S(1)} %bitcast.135, s32[128,12]{0,1:T(8,128)S(1)} %copy.16, f32[4,1536]{1,0:T(4,128)S(1)} %collective-permute-done.1, f32[4,1536]{1,0:T(4,128)S(1)} %dynamic-slice_bitcast_fusion, pred[]{:T(512)S(6)} %eq.36), kind=kOutput, calls=%fused_computation.28 | convolution fusion | flops 268996608 | bytes 110593 | tf_op jit(solution)/shard_map/pc,gkc->gpk/dot_general | solution.py:80
  935.7 23.7 %all_to_all.32 = f32[128,4,12]{2,1,0:T(4,128)S(1)} all-to-all(f32[128,4,12]{2,1,0:T(4,128)S(1)} %copy.29), channel_id=1, replica_groups=mesh['period'=128,'half'=2] {'period'}, dimensions={0} | all-to-all | bytes 49152 | tf_op jit(solution)/shard_map/all_to_all | solution.py:82
  960.2 17.2 %all_to_all.33 = bf16[128,4,12]{2,1,0:T(4,128)(2,1)S(1)} all-to-all(bf16[128,4,12]{2,1,0:T(4,128)(2,1)S(1)} %copy.31), channel_id=1, replica_groups=mesh['period'=128,'half'=2] {'period'}, dimensions={0} | all-to-all | bytes 24576 | tf_op jit(solution)/shard_map/all_to_all | solution.py:58
  978.0 43.1 %all_to_all.34 = bf16[128,1,4,1536]{3,2,1,0:T(4,128)(2,1)} all-to-all(bf16[128,1,4,1536]{3,2,1,0:T(4,128)(2,1)S(1)} %stack.24), channel_id=1, replica_groups=mesh['period'=128,'half'=2] {'period'}, dimensions={0} | all-to-all | bytes 3145728 | tf_op jit(solution)/shard_map/all_to_all | solution.py:90
  1021.2 3.9 copy.33
  1025.0 2.0 fusion.68
  1029.0 0.7 copy.48
  1029.7 1.3 reshape.132
  1031.1 13.0 %reduce-scatter.9.cloned.1.call-done = bf16[256,32]{1,0:T(8,128)(2,1)} async-done(((bf16[512,32]{1,0:T(8,128)(2,1)}), bf16[256,32]{1,0:T(8,128)(2,1)}) %reduce-scatter.9.cloned.1.call-update) | async-done | bytes 16400
  1044.0 1.2 reshape.133
  1045.8 77.4 %psum.38 = f32[4]{0:T(128)S(1)} all-reduce(f32[4]{0:T(128)S(1)} %multiply_reduce_fusion.1), channel_id=1, replica_groups=mesh['period'=128,'half'=2] {'period','half'}, use_global_device_ids=true, to_apply=%region_11.12 | all-reduce | flops 4 | bytes 32 | tf_op jit(solution)/shard_map/psum | solution.py:114
  1123.2 0.8 multiply_reduce_fusion
  1124.0 73.1 %psum.39 = f32[4]{0:T(128)S(1)} all-reduce(f32[4]{0:T(128)S(1)} %get-tuple-element.4), channel_id=1, replica_groups=mesh['period'=128,'half'=2] {'period','half'}, use_global_device_ids=true, to_apply=%region_13.14 | all-reduce | flops 4 | bytes 32 | tf_op jit(solution)/shard_map/psum | solution.py:117
  (65 shorter events, 10.9 us)
Async XLA Ops:
  7.2 87.3 %copy-start = (bf16[8,512,256]{2,1,0:T(8,128)(2,1)S(1)}, bf16[8,512,256]{2,1,0:T(8,128)(2,1)}, u32[]{:S(2)}) copy-start(bf16[8,512,256]{2,1,0:T(8,128)(2,1)} %param.8) | copy-start | bytes 6291460
  7.2 88.5 %copy-start.3 = (s32[8,4]{0,1:T(4,128)S(1)}, s32[8,4]{0,1:T(4,128)}, u32[]{:S(2)}) copy-start(s32[8,4]{0,1:T(4,128)} %param.10) | copy-start | bytes 388
  7.2 320.7 %all-reduce.5.cloned.1.call-start = ((), (), s32[]{:S(2)}) async-start(), calls=%async_computation.10 | async-start | bytes 6291456
  105.2 0.7 copy-start.5
  105.2 229.1 %copy-start.2 = (s32[2,3072]{1,0:T(2,128)S(1)}, s32[2,3072]{1,0:T(2,128)}, u32[]{:S(2)}) copy-start(s32[2,3072]{1,0:T(2,128)} %param.12) | copy-start | bytes 73732
  329.3 5.8 collective-permute-start
  335.1 70.5 %copy-start.1 = (f32[128,128]{1,0:T(8,128)S(1)}, f32[128,128]{1,0:T(8,128)}, u32[]{:S(2)}) copy-start(f32[128,128]{1,0:T(8,128)} %param.13) | copy-start | bytes 196612
  381.9 50.9 %copy-start.4 = (f32[8,4]{0,1:T(4,128)S(1)}, f32[8,4]{0,1:T(4,128)}, u32[]{:S(2)}) copy-start(f32[8,4]{0,1:T(4,128)} %param.9) | copy-start | bytes 388
  425.4 44.0 %all-to-all-start.2 = ((bf16[128,1,4,1536]{3,2,1,0:T(4,128)(2,1)}), bf16[128,1,4,1536]{3,2,1,0:T(4,128)(2,1)}, u32[]{:S(2)}, u32[]{:S(2)}) async-start(bf16[128,1,4,1536]{3,2,1,0:T(4,128)(2,1)} %stack.21), calls=%async_computation.2 | async-start | bytes 3145728 | tf_op jit(solution)/shard_map/all_to_all | solution.py:90
  432.8 59.4 %reduce-scatter.7.cloned.1.call-start = ((), (), s32[]{:S(2)}) async-start(), calls=%async_computation.8 | async-start | bytes 196608
  479.3 402.3 %all-reduce.7.cloned.1.call-start = ((), (), s32[]{:S(2)}) async-start(), calls=%async_computation.11 | async-start | bytes 6291456
  657.7 386.4 %reduce-scatter.9.cloned.1.call-start = ((), (), s32[]{:S(2)}) async-start(), calls=%async_computation.9 | async-start | bytes 196608
  882.9 6.0 collective-permute-start.1
Sparse Core Ops, SparseCore 0:
  105.3 222.5 all-reduce.4
  479.4 12.7 reduce-scatter.6
  657.8 223.6 all-reduce.6
  1031.2 12.7 reduce-scatter.8
